TPU v7x, 512 devices: a whole 4x4x16 slice. The times are simulated.
512 devices in a mesh: expert: 8 (over z_hi, x), shard: 64 (over y, z_lo, core).
Axes of the slice: x: 4, y: 4, z: 16 (z_hi: 2, z_lo: 8; z = z_hi * 8 + z_lo), core: 2. Of those that a mesh axis runs over, the one named last changes fastest.
Arguments:
- tokens: bfloat16 [1024, 2048], P('expert', 'shard'), may hold values from -6 to 6
- cotangent: bfloat16 [1024, 2048], P('expert', 'shard'), may hold values from -6 to 6
- expert_ids: int32 [1024, 2], P('expert'), may hold values from 0 to 7, all different within a row; in each aligned block of 128 rows (0 to 127, 128 to 255, ...) at most 48 rows name the same one
- route_weights: float32 [1024, 2], P('expert'), may hold values from 0.2 to 1
- dense_gate: bfloat16 [2048, 11008], P('expert', 'shard'), may hold values from -0.125 to 0.125
- dense_up: bfloat16 [2048, 11008], P('expert', 'shard'), may hold values from -0.125 to 0.125
- dense_down: bfloat16 [11008, 2048], P('shard', 'expert'), may hold values from -0.15625 to 0.15625
- noise_gate: bfloat16 [8, 2048, 1280], P('expert', None, 'shard'), may hold values from -0.125 to 0.125
- noise_up: bfloat16 [8, 2048, 1280], P('expert', None, 'shard'), may hold values from -0.125 to 0.125
- noise_down: bfloat16 [8, 1280, 2048], P('expert', 'shard'), may hold values from -0.0546875 to 0.0546875
Outputs:
- mixed: bfloat16 [1024, 2048], P('expert', 'shard')
- grad_gate: bfloat16 [8, 12288, 2048], P('expert', 'shard')
- grad_up: bfloat16 [8, 12288, 2048], P('expert', 'shard')
- grad_down: bfloat16 [8, 12288, 2048], P('expert', 'shard')
Inputs may be any that keep to these rules, and one draw needn't show every extreme that they name: `expert_ids`: the two experts of a token differ. Within each aligned block of 128 tokens no expert is named by more than 48 tokens, a bound that some block reaches.
All inputs are finite; a program needn't handle non-finite values.
Results may differ from a plain program's by a relative error of at most 0.0058.
Values may be sent and summed in bfloat16 or wider, within the bound.
No kernel may reach another device: no remote copies, remote signals or barrier semaphores. Data moves between devices by JAX's collectives and lax.ppermute only.
A program may use at most 64 MiB of HBM per device.

v0:
```python
import jax
import jax.numpy as jnp
from jax import lax
from jax.sharding import PartitionSpec as P


def local(
    tokens,
    cotangent,
    expert_ids,
    route_weights,
    dense_gate,
    dense_up,
    dense_down,
    noise_gate,
    noise_up,
    noise_down,
):
    experts = lax.axis_size("expert")
    tok_dev = tokens.shape[0]
    capacity = min(tok_dev, 3 * tok_dev // experts)
    rows_total = experts * capacity
    gate_full, up_full = (
        lax.all_gather(dense_gate, "expert", axis=0, tiled=True),
        lax.all_gather(dense_up, "expert", axis=0, tiled=True),
    )
    down_full = lax.all_gather(dense_down, "expert", axis=1, tiled=True)
    wide_gate = jnp.concatenate([gate_full, noise_gate[0]], axis=1)
    wide_up = jnp.concatenate([up_full, noise_up[0]], axis=1)
    wide_down = jnp.concatenate([down_full, noise_down[0]], axis=0)
    pair_ids = expert_ids.reshape(-1)
    onehot = (pair_ids[:, None] == jnp.arange(experts, dtype=jnp.int32)[None, :]).astype(jnp.int32)
    earlier = jnp.cumsum(onehot, axis=0) - onehot
    slot_index = jnp.sum(earlier * onehot, axis=1)
    target = pair_ids * capacity + slot_index
    flat_weights = route_weights.reshape(-1)
    row_width = tokens.shape[1]
    tok_pairs = jnp.repeat(tokens, 2, axis=0)
    cot_pairs = (
        flat_weights[:, None] * jnp.repeat(cotangent, 2, axis=0).astype(jnp.float32)
    ).astype(jnp.bfloat16)
    send_tok = jnp.zeros((rows_total, row_width), jnp.bfloat16).at[target].set(tok_pairs)
    send_cot = jnp.zeros((rows_total, row_width), jnp.bfloat16).at[target].set(cot_pairs)
    send_tok, send_cot = (send_tok, send_cot)
    slot_tok, slot_cot = (
        lax.all_to_all(send_tok, "expert", split_axis=0, concat_axis=0, tiled=True),
        lax.all_to_all(send_cot, "expert", split_axis=0, concat_axis=0, tiled=True),
    )
    inputs, slot_grads = (
        lax.all_gather(slot_tok, "shard", axis=1, tiled=True),
        lax.all_gather(slot_cot, "shard", axis=1, tiled=True),
    )
    gate_pre = jnp.dot(inputs, wide_gate, preferred_element_type=jnp.float32)
    up_pre = jnp.dot(inputs, wide_up, preferred_element_type=jnp.float32)
    sigmoid_gate = jax.nn.sigmoid(gate_pre)
    silu_gate = gate_pre * sigmoid_gate
    hidden = (silu_gate * up_pre).astype(jnp.bfloat16)
    summed = lax.psum_scatter(
        lax.dot_general(
            wide_down, hidden, (((0,), (1,)), ((), ())), preferred_element_type=jnp.float32
        ),
        "shard",
        scatter_dimension=0,
        tiled=True,
    )
    out_slots = summed.astype(jnp.bfloat16)
    returned = lax.all_to_all(out_slots, "expert", split_axis=1, concat_axis=1, tiled=True)
    picked = jnp.take(returned, target, axis=1).astype(jnp.float32)
    weighted = (picked * flat_weights[None, :]).reshape(picked.shape[0], tok_dev, 2)
    mixed = jnp.sum(weighted, axis=2).T.astype(jnp.bfloat16)
    grad_hidden = lax.dot_general(
        slot_grads, wide_down, (((1,), (1,)), ((), ())), preferred_element_type=jnp.float32
    )
    grad_gate_pre = (
        grad_hidden * up_pre * sigmoid_gate * (1.0 + gate_pre * (1.0 - sigmoid_gate))
    ).astype(jnp.bfloat16)
    grad_up_pre = (grad_hidden * silu_gate).astype(jnp.bfloat16)
    contract_rows = (((0,), (0,)), ((), ()))
    grad_gate = lax.dot_general(
        grad_gate_pre, inputs, contract_rows, preferred_element_type=jnp.float32
    ).astype(jnp.bfloat16)
    grad_up = lax.dot_general(
        grad_up_pre, inputs, contract_rows, preferred_element_type=jnp.float32
    ).astype(jnp.bfloat16)
    grad_down = lax.dot_general(
        hidden, slot_grads, contract_rows, preferred_element_type=jnp.float32
    ).astype(jnp.bfloat16)
    return (mixed, grad_gate[None], grad_up[None], grad_down[None])


def solution(mesh):
    in_specs = (
        P("expert", "shard"),
        P("expert", "shard"),
        P("expert", None),
        P("expert", None),
        P("expert", "shard"),
        P("expert", "shard"),
        P("shard", "expert"),
        P("expert", None, "shard"),
        P("expert", None, "shard"),
        P("expert", "shard", None),
    )
    out_specs = (
        P("expert", "shard"),
        P("expert", "shard", None),
        P("expert", "shard", None),
        P("expert", "shard", None),
    )
    return jax.shard_map(local, mesh=mesh, in_specs=in_specs, out_specs=out_specs, check_vma=False)
```

profile of v0, /device:TPU:2, one launch (start us, length us, event | category | flops | bytes accessed | tf_op | source)
XLA Modules:
  0.0 763.7 jit_solution(14176948831567929491)
XLA Ops:
  7.2 0.7 broadcast_multiply_fusion
  7.9 0.8 copy.65
  9.2 0.6 reduce-window.6
  10.1 0.8 copy.70
  11.1 1.2 scatter_custom_fusion
  12.5 31.4 %all_to_all.36 = bf16[8,2,768]{2,1,0:T(2,128)(2,1)S(1)} all-to-all(bf16[8,2,768]{2,1,0:T(2,128)(2,1)S(1)} %reshape.120), channel_id=1, replica_groups=mesh['expert'=8,'shard'=64] {'expert'}, dimensions={0} | all-to-all | bytes 49152 | tf_op jit(solution)/shard_map/all_to_all | solution.py:46
  44.1 0.7 all_to_all.26
  44.8 0.8 copy.76
  45.6 0.8 copy.78
  46.6 1.3 scatter_custom_fusion.1
  48.2 17.3 %all_to_all.37 = bf16[8,2,768]{2,1,0:T(2,128)(2,1)S(1)} all-to-all(bf16[8,2,768]{2,1,0:T(2,128)(2,1)S(1)} %reshape.124), channel_id=1, replica_groups=mesh['expert'=8,'shard'=64] {'expert'}, dimensions={0} | all-to-all | bytes 49152 | tf_op jit(solution)/shard_map/all_to_all | solution.py:47
  65.6 0.7 all_to_all.32
  66.4 56.7 %all_gather.17 = bf16[2048,172]{0,1:T(8,128)(2,1)} all-gather(bf16[256,172]{0,1:T(8,128)(2,1)S(1)} %copy-done.4), channel_id=1, replica_groups=mesh['expert'=8,'shard'=64] {'expert'}, dimensions={0}, use_global_device_ids=true | all-gather | bytes 792576 | tf_op jit(solution)/shard_map/all_gather | solution.py:24
  123.2 67.1 %all_gather.18 = bf16[2048,172]{0,1:T(8,128)(2,1)S(1)} all-gather(bf16[256,172]{0,1:T(8,128)(2,1)S(1)} %copy-done.5), channel_id=1, replica_groups=mesh['expert'=8,'shard'=64] {'expert'}, dimensions={0}, use_global_device_ids=true | all-gather | bytes 792576 | tf_op jit(solution)/shard_map/all_gather | solution.py:25
  190.3 74.2 %all_gather.15 = bf16[172,2048]{1,0:T(8,128)(2,1)S(1)} all-gather(bf16[172,256]{1,0:T(8,128)(2,1)S(1)} %copy-done.6), channel_id=1, replica_groups=mesh['expert'=8,'shard'=64] {'expert'}, dimensions={1}, use_global_device_ids=true | all-gather | bytes 792576 | tf_op jit(solution)/shard_map/all_gather | solution.py:27
  264.5 2.4 fusion.3
  266.9 1.3 multiply_convert_fusion.2
  268.2 3.3 fusion.12
  271.8 0.5 copy-done.7
  272.4 11.0 %all-gather.5.cloned.1.call-done = bf16[384,2048]{0,1:T(8,128)(2,1)} async-done(((bf16[384,32]{0,1:T(8,128)(2,1)}), bf16[384,2048]{0,1:T(8,128)(2,1)}) %all-gather.5.cloned.1.call-update) | async-done | bytes 1572880 | tf_op jit(solution)/shard_map/all_gather | solution.py:51
  283.5 2.0 fusion.11
  285.4 1.6 fusion.1
  287.1 1.6 fusion
  288.7 442.6 %reduce-scatter.2.cloned.1.call-done = f32[32,384]{1,0:T(8,128)} async-done(((f32[2048,384]{1,0:T(8,128)}), f32[32,384]{1,0:T(8,128)}) %reduce-scatter.2.cloned.1.call-update) | async-done | bytes 49168 | tf_op jit(solution)/shard_map/reduce_scatter | solution.py:58
  731.2 0.8 convert_element_type.51
  732.2 0.7 reshape.122
  732.9 8.6 %all-to-all-start.1 = ((bf16[8,2,768]{2,1,0:T(2,128)(2,1)}), bf16[8,2,768]{2,1,0:T(2,128)(2,1)S(1)}, u32[]{:S(2)}, u32[]{:S(2)}) async-start(bf16[8,2,768]{2,1,0:T(2,128)(2,1)} %reshape.122), calls=%async_computation.2 | async-start | bytes 49152 | tf_op jit(solution)/shard_map/all_to_all | solution.py:67
  741.5 2.5 fusion.2
  744.0 11.0 %all-to-all-done.1 = bf16[8,2,768]{2,1,0:T(2,128)(2,1)S(1)} async-done(((bf16[8,2,768]{2,1,0:T(2,128)(2,1)}), bf16[8,2,768]{2,1,0:T(2,128)(2,1)S(1)}, u32[]{:S(2)}, u32[]{:S(2)}) %all-to-all-start.1) | async-done | bytes 24608 | tf_op jit(solution)/shard_map/all_to_all | solution.py:67
  755.3 0.9 gather_fusion
  756.1 0.4 multiply_reduce_fusion
  756.5 0.7 copy.82
  (54 shorter events, 2.8 us)
Async XLA Ops:
  7.2 59.3 %copy-start.4 = (bf16[256,172]{0,1:T(8,128)(2,1)S(1)}, bf16[256,172]{0,1:T(8,128)(2,1)}, u32[]{:S(2)}) copy-start(bf16[256,172]{0,1:T(8,128)(2,1)} %param.14) | copy-start | bytes 264196
  7.2 257.3 %all-gather.3.cloned.1.call-start = ((), (), s32[]{:S(2)}) async-start(), calls=%async_computation.4 | async-start | bytes 1597440 | tf_op jit(solution)/shard_map/all_gather | solution.py:50
  9.0 114.2 %copy-start.5 = (bf16[256,172]{0,1:T(8,128)(2,1)S(1)}, bf16[256,172]{0,1:T(8,128)(2,1)}, u32[]{:S(2)}) copy-start(bf16[256,172]{0,1:T(8,128)(2,1)} %param.15) | copy-start | bytes 264196
  44.0 146.3 %copy-start.6 = (bf16[172,256]{1,0:T(8,128)(2,1)S(1)}, bf16[172,256]{1,0:T(8,128)(2,1)}, u32[]{:S(2)}) copy-start(bf16[172,256]{1,0:T(8,128)(2,1)} %param.16) | copy-start | bytes 264196
  44.8 238.7 %all-gather.5.cloned.1.call-start = ((), (), s32[]{:S(2)}) async-start(), calls=%async_computation.6 | async-start | bytes 1597440 | tf_op jit(solution)/shard_map/all_gather | solution.py:51
  66.4 664.8 %reduce-scatter.2.cloned.1.call-start = ((), (), s32[]{:S(2)}) async-start(), calls=%async_computation.5 | async-start | bytes 3194880 | tf_op jit(solution)/shard_map/reduce_scatter | solution.py:58
  264.5 2.4 copy-start
  264.5 2.4 copy-start.8
  266.9 1.4 copy-start.3
  271.6 0.7 copy-start.7
  285.4 1.6 copy-start.2
  287.1 454.5 %copy-start.1 = (bf16[384,2048]{0,1:T(8,128)(2,1)S(1)}, bf16[384,2048]{0,1:T(8,128)(2,1)}, u32[]{:S(2)}) copy-start(bf16[384,2048]{0,1:T(8,128)(2,1)} %all-gather.5.cloned.1.call-done) | copy-start | bytes 4718596
  732.9 22.1 %all-to-all-start.1 = ((bf16[8,2,768]{2,1,0:T(2,128)(2,1)}), bf16[8,2,768]{2,1,0:T(2,128)(2,1)S(1)}, u32[]{:S(2)}, u32[]{:S(2)}) async-start(bf16[8,2,768]{2,1,0:T(2,128)(2,1)} %reshape.122), calls=%async_computation.2 | async-start | bytes 49152 | tf_op jit(solution)/shard_map/all_to_all | solution.py:67
Sparse Core Ops, SparseCore 0:
  44.9 113.7 all-gather.2
  161.5 121.9 all-gather.4
  286.3 444.9 reduce-scatter.1
where the time goes:
time: 764 us
  waiting for transfers between devices  465 us (61%)
  blocking collectives  247 us (32%)
  matrix products  14.7 us (2%)
  between operations  14 us (2%)
  local copies, waits for them, and re-layouts  11 us (1%)
  starting transfers between devices  8.76 us (1%)
    reduce_scatter x1, waiting for transfers between devices, local(): lax.psum_scatter(lax.dot_general(wide_down, hidden, (((0,), (1,)), ((), (...  443 us
    all_gather x1, blocking collectives, local(): down_full = lax.all_gather(dense_down, 'expert', axis=1, tiled=True)  74.2 us
    all_gather x1, blocking collectives, local(): lax.all_gather(dense_up, 'expert', axis=0, tiled=True)  67.1 us
    all_gather x1, blocking collectives, local(): lax.all_gather(dense_gate, 'expert', axis=0, tiled=True)  56.7 us
    all_to_all x1, blocking collectives, local(): lax.all_to_all(send_tok, 'expert', split_axis=0, concat_axis=0, tiled=True)  31.4 us
    all_to_all x1, blocking collectives, local(): lax.all_to_all(send_cot, 'expert', split_axis=0, concat_axis=0, tiled=True)  17.3 us
  transfers between devices with their start and end apart: 4, of which 3 were waited for; matrix products, arithmetic and copies ran while one was open for 2% of the time, Pallas kernels for 0%

commit v1 on v0

--- a/solution.py
+++ b/solution.py
@@ -22,7 +22,9 @@
     rows_total = experts * capacity
     gate_full, up_full = (
         lax.all_gather(dense_gate, "expert", axis=0, tiled=True),
-        lax.all_gather(dense_up, "expert", axis=0, tiled=True),
+        jnp.concatenate(
+            lax.all_to_all(jnp.stack([dense_up] * lax.axis_size("expert")), "expert", 0, 0), axis=0
+        ),
     )
     down_full = lax.all_gather(dense_down, "expert", axis=1, tiled=True)
     wide_gate = jnp.concatenate([gate_full, noise_gate[0]], axis=1)

time: 764 us -> 797 us (1.043)
  waiting for transfers between devices: 465 us -> 526 us
  blocking collectives: 247 us -> 213 us
    all_gather x1, waiting for transfers between devices: 11 us -> 80.7 us  [local(): lax.all_gather(slot_cot, 'shard', axis=1, tiled=True)]
    all_gather x1 -> x0, blocking collectives: 67.1 us -> none  [local(): lax.all_gather(dense_up, 'expert', axis=0, tiled=True)]
    all_gather x1, blocking collectives: 56.7 us -> 84.1 us  [local(): lax.all_gather(dense_gate, 'expert', axis=0, tiled=True)]
  transfers between devices with their start and end apart: 4 -> 5, of which waited for: 3 -> 3; matrix products, arithmetic and copies ran while one was open for 2% -> 2% of each run, Pallas kernels for 0% -> 0%
where the time goes in v1:
time: 797 us; the launch traced here: 796 us
  waiting for transfers between devices  526 us (66%)
  blocking collectives  213 us (27%)
  between operations  14 us (2%)
  local copies, waits for them, and re-layouts  13.5 us (2%)
  matrix products  13.3 us (2%)
  starting transfers between devices  12.8 us (2%)
    reduce_scatter x1, waiting for transfers between devices, local(): lax.psum_scatter(lax.dot_general(wide_down, hidden, (((0,), (1,)), ((), (...  435 us
    all_gather x1, blocking collectives, local(): lax.all_gather(dense_gate, 'expert', axis=0, tiled=True)  84.1 us
    all_gather x1, waiting for transfers between devices, local(): lax.all_gather(slot_cot, 'shard', axis=1, tiled=True)  80.7 us
    all_gather x1, blocking collectives, local(): down_full = lax.all_gather(dense_down, 'expert', axis=1, tiled=True)  79.9 us
    all_to_all x1, blocking collectives, local(): lax.all_to_all(send_tok, 'expert', split_axis=0, concat_axis=0, tiled=True)  31.4 us
    all_to_all x1, blocking collectives, local(): lax.all_to_all(send_cot, 'expert', split_axis=0, concat_axis=0, tiled=True)  17.3 us
  transfers between devices with their start and end apart: 5, of which 3 were waited for; matrix products, arithmetic and copies ran while one was open for 2% of the time, Pallas kernels for 0%

profile of v1, /device:TPU:2, one launch (start us, length us, event | category | flops | bytes accessed | tf_op | source)
XLA Modules:
  0.0 796.1 jit_solution(16748841665362500584)
XLA Ops:
  7.2 0.7 broadcast_multiply_fusion
  7.9 0.8 copy.72
  9.2 0.6 reduce-window.6
  10.1 0.8 copy.77
  11.0 1.2 scatter_custom_fusion
  12.5 31.4 %all_to_all.41 = bf16[8,2,768]{2,1,0:T(2,128)(2,1)S(1)} all-to-all(bf16[8,2,768]{2,1,0:T(2,128)(2,1)S(1)} %reshape.126), channel_id=1, replica_groups=mesh['expert'=8,'shard'=64] {'expert'}, dimensions={0} | all-to-all | bytes 49152 | tf_op jit(solution)/shard_map/all_to_all | solution.py:48
  44.0 0.7 all_to_all.29
  44.8 0.8 copy.84
  45.6 0.8 copy.86
  46.6 1.3 scatter_custom_fusion.1
  48.1 17.3 %all_to_all.42 = bf16[8,2,768]{2,1,0:T(2,128)(2,1)S(1)} all-to-all(bf16[8,2,768]{2,1,0:T(2,128)(2,1)S(1)} %reshape.130), channel_id=1, replica_groups=mesh['expert'=8,'shard'=64] {'expert'}, dimensions={0} | all-to-all | bytes 49152 | tf_op jit(solution)/shard_map/all_to_all | solution.py:49
  65.4 0.9 stack.2
  66.3 4.9 all-to-all-start.1
  71.4 0.7 all_to_all.36
  72.2 84.1 %all_gather.14 = bf16[2048,172]{0,1:T(8,128)(2,1)S(1)} all-gather(bf16[256,172]{0,1:T(8,128)(2,1)S(1)} %copy-done.4), channel_id=1, replica_groups=mesh['expert'=8,'shard'=64] {'expert'}, dimensions={0}, use_global_device_ids=true | all-gather | bytes 792576 | tf_op jit(solution)/shard_map/all_gather | solution.py:24
  156.3 79.9 %all_gather.12 = bf16[172,2048]{1,0:T(8,128)(2,1)S(1)} all-gather(bf16[172,256]{1,0:T(8,128)(2,1)S(1)} %copy-done.5), channel_id=1, replica_groups=mesh['expert'=8,'shard'=64] {'expert'}, dimensions={1}, use_global_device_ids=true | all-gather | bytes 792576 | tf_op jit(solution)/shard_map/all_gather | solution.py:29
  236.5 1.0 copy.95
  237.6 2.1 fusion.3
  239.7 0.6 multiply_convert_fusion.2
  240.6 2.4 fusion.12
  243.9 80.7 %all-gather.5.cloned.1.call-done = bf16[384,2048]{0,1:T(8,128)(2,1)} async-done(((bf16[384,32]{0,1:T(8,128)(2,1)}), bf16[384,2048]{0,1:T(8,128)(2,1)}) %all-gather.5.cloned.1.call-update) | async-done | bytes 1572880 | tf_op jit(solution)/shard_map/all_gather | solution.py:53
  324.5 2.0 fusion.11
  326.5 1.6 fusion.1
  328.1 1.6 fusion
  329.7 434.7 %reduce-scatter.2.cloned.1.call-done = f32[32,384]{1,0:T(8,128)} async-done(((f32[2048,384]{1,0:T(8,128)}), f32[32,384]{1,0:T(8,128)}) %reduce-scatter.2.cloned.1.call-update) | async-done | bytes 49168 | tf_op jit(solution)/shard_map/reduce_scatter | solution.py:60
  764.5 0.8 convert_element_type.51
  765.4 0.7 reshape.128
  766.1 7.8 all-to-all-start.2
  773.9 3.0 fusion.2
  776.9 10.5 %all-to-all-done.2 = bf16[8,2,768]{2,1,0:T(2,128)(2,1)S(1)} async-done(((bf16[8,2,768]{2,1,0:T(2,128)(2,1)}), bf16[8,2,768]{2,1,0:T(2,128)(2,1)S(1)}, u32[]{:S(2)}, u32[]{:S(2)}) %all-to-all-start.2) | async-done | bytes 24608 | tf_op jit(solution)/shard_map/all_to_all | solution.py:69
  787.6 0.9 gather_fusion
  788.9 0.7 copy.90
  (59 shorter events, 4.1 us)
Async XLA Ops:
  7.2 58.3 %copy-start.3 = (bf16[256,172]{0,1:T(8,128)(2,1)S(1)}, bf16[256,172]{0,1:T(8,128)(2,1)}, u32[]{:S(2)}) copy-start(bf16[256,172]{0,1:T(8,128)(2,1)} %param.15) | copy-start | bytes 264196
  7.2 230.4 %all-gather.3.cloned.1.call-start = ((), (), s32[]{:S(2)}) async-start(), calls=%async_computation.5 | async-start | bytes 1597440 | tf_op jit(solution)/shard_map/all_gather | solution.py:52
  46.5 25.6 %copy-start.4 = (bf16[256,172]{0,1:T(8,128)(2,1)S(1)}, bf16[256,172]{0,1:T(8,128)(2,1)}, u32[]{:S(2)}) copy-start(bf16[256,172]{0,1:T(8,128)(2,1)} %param.14) | copy-start | bytes 264196
  65.4 90.8 %copy-start.5 = (bf16[172,256]{1,0:T(8,128)(2,1)S(1)}, bf16[172,256]{1,0:T(8,128)(2,1)}, u32[]{:S(2)}) copy-start(bf16[172,256]{1,0:T(8,128)(2,1)} %param.16) | copy-start | bytes 264196
  66.3 169.9 %all-to-all-start.1 = ((bf16[8,256,172]{1,2,0:T(8,128)(2,1)}), bf16[8,256,172]{1,2,0:T(8,128)(2,1)S(1)}, u32[]{:S(2)}, u32[]{:S(2)}) async-start(bf16[8,256,172]{1,2,0:T(8,128)(2,1)} %stack.2), calls=%async_computation.1 | async-start | bytes 1441792 | tf_op jit(solution)/shard_map/all_to_all | solution.py:26
  71.2 253.3 %all-gather.5.cloned.1.call-start = ((), (), s32[]{:S(2)}) async-start(), calls=%async_computation.7 | async-start | bytes 1597440 | tf_op jit(solution)/shard_map/all_gather | solution.py:53
  72.1 692.3 %reduce-scatter.2.cloned.1.call-start = ((), (), s32[]{:S(2)}) async-start(), calls=%async_computation.6 | async-start | bytes 3194880 | tf_op jit(solution)/shard_map/reduce_scatter | solution.py:60
  236.4 1.1 copy-start.7
  237.5 2.1 copy-start
  237.5 2.2 copy-start.1
  237.5 2.2 copy-start.8
  239.7 0.9 copy-start.2
  243.0 0.7 copy-start.6
  766.1 21.3 %all-to-all-start.2 = ((bf16[8,2,768]{2,1,0:T(2,128)(2,1)}), bf16[8,2,768]{2,1,0:T(2,128)(2,1)S(1)}, u32[]{:S(2)}, u32[]{:S(2)}) async-start(bf16[8,2,768]{2,1,0:T(2,128)(2,1)} %reshape.128), calls=%async_computation.3 | async-start | bytes 49152 | tf_op jit(solution)/shard_map/all_to_all | solution.py:69
Sparse Core Ops, SparseCore 0:
  44.9 142.0 all-gather.2
  189.8 134.7 all-gather.4
  327.3 437.0 reduce-scatter.1
